TPU v7x, 128 devices: a whole 4x4x4 slice. The times are simulated.
128 devices in a mesh: judge: 4 (over y_hi, core), fsdp: 32 (over y_lo, x, z).
Axes of the slice: x: 4, y: 4 (y_hi: 2, y_lo: 2; y = y_hi * 2 + y_lo), z: 4, core: 2. Of those that a mesh axis runs over, the one named last changes fastest.
Arguments:
- hidden: bfloat16 [4, 32768, 4096], P('judge', 'fsdp'), may hold values from -32 to 32
- lengths: int32 [64], replicated, may hold values from 128 to 512
- duplicate_group_index: int32 [64], replicated, may hold values from 0 to 15, as said below
- attn_gain: bfloat16 [4, 4096], P('judge', 'fsdp'), may hold values from 0.5 to 1.5
- w_query: bfloat16 [4, 4096, 4096], P('judge', None, 'fsdp'), may hold values from -1 to 1
- w_key: bfloat16 [4, 4096, 1024], P('judge', 'fsdp'), may hold values from -1 to 1
- w_value: bfloat16 [4, 4096, 1024], P('judge', 'fsdp'), may hold values from -0.09375 to 0.09375
- w_out: bfloat16 [4, 4096, 4096], P('judge', 'fsdp'), may hold values from -0.09375 to 0.09375
- mlp_gain: bfloat16 [4, 4096], P('judge', 'fsdp'), may hold values from 0.5 to 1.5
- w_gate: bfloat16 [4, 4096, 14336], P('judge', None, 'fsdp'), may hold values from -0.09375 to 0.09375
- w_up: bfloat16 [4, 4096, 14336], P('judge', None, 'fsdp'), may hold values from -0.09375 to 0.09375
- w_down: bfloat16 [4, 14336, 4096], P('judge', 'fsdp'), may hold values from -0.046875 to 0.046875
- final_gain: bfloat16 [4, 4096], P('judge', 'fsdp'), may hold values from 0.5 to 1.5
- reward_head: float32 [4, 4096], P('judge'), may hold values from -8 to 8
Outputs:
- survivor_weights: float32 [64], replicated
- cluster_features: float32 [16, 4096], P(None, 'fsdp')
Inputs may be any that keep to these rules, and one draw needn't show every extreme that they name: `duplicate_group_index`: every cluster holds exactly four candidates.
All inputs are finite; a program needn't handle non-finite values.
Results may differ from a plain program's by a relative error of at most 0.003.
Values may be sent and summed in bfloat16 or wider, within the bound.
No kernel may reach another device: no remote copies, remote signals or barrier semaphores. Data moves between devices by JAX's collectives and lax.ppermute only.
A program may use at most 192 MiB of HBM per device.

v0:
```python
import math
import jax
import jax.numpy as jnp
from jax import lax
from jax.sharding import PartitionSpec as P

KV_HEADS = 8
HEAD_DIM = 128
LEN = 512
EPS = 1e-05
ROPE_BASE = 500000.0


def in_order(blocks, dim):
    dims = list(blocks.shape[1:])
    dims[dim] *= blocks.shape[0]
    return jnp.moveaxis(blocks, 0, dim).reshape(dims)


def gather_packed(arrays, axis, dims):
    ravelled = jnp.concatenate([a.reshape(-1) for a in arrays])
    lines, at, done = (lax.all_gather(ravelled, axis), 0, [])
    for a, dim in zip(arrays, dims):
        blocks = lines[:, at : at + a.size].reshape(-1, *a.shape)
        done.append(in_order(blocks, dim))
        at += a.size
    return tuple(done)


def sent_together(arrays, axis, dim, along):
    both = jnp.concatenate(arrays, axis=along)
    filled, at, done = (lax.all_gather(both, axis, axis=dim, tiled=True), 0, [])
    for a in arrays:
        done.append(lax.slice_in_dim(filled, at, at + a.shape[along], axis=along))
        at += a.shape[along]
    return tuple(done)


def cut_along(x, dim, peers):
    before, after = (x.shape[:dim], x.shape[dim + 1 :])
    return jnp.moveaxis(x.reshape(*before, peers, -1, *after), dim, 0)


def sum_at_owner(x, axis, dim):
    peers = lax.axis_size(axis)
    blocks = lax.all_to_all(cut_along(x, dim, peers), axis, 0, 0, tiled=True)
    return jnp.sum(blocks, axis=0)


def rows_for(lines, peers):
    spare = -lines.shape[0] % peers
    if not spare:
        return lines
    return jnp.concatenate([lines, jnp.zeros((spare, *lines.shape[1:]), lines.dtype)])


def from_everyone(x, axis):
    peers = lax.axis_size(axis)
    return lax.all_to_all(jnp.broadcast_to(x[None], (peers, *x.shape)), axis, 0, 0, tiled=True)


def gather_directly(x, axis, dim):
    blocks = from_everyone(x, axis)
    return in_order(blocks, dim)


def total_of(x, axes):
    lines = x.reshape(-1, x.shape[-1])
    own = sum_at_owner(rows_for(lines, lax.axis_size(axes)), axes, 0)
    whole = gather_directly(own, axes, 0)
    return whole[: len(lines)].reshape(x.shape)


def taken_together(x, axis):
    return from_everyone(x, axis).sum(axis=0)


def packed_total(arrays, axis):
    ends = [0]
    for a in arrays:
        ends.append(ends[-1] + a.size)
    running = taken_together(jnp.concatenate([a.ravel() for a in arrays]), axis)
    return tuple((running[b:e].reshape(a.shape) for a, b, e in zip(arrays, ends, ends[1:])))


def row_scale(v):
    return lax.rsqrt(jnp.mean(v * v, axis=-1, keepdims=True) + EPS)


def angles(position):
    half = HEAD_DIM // 2
    freq = jnp.exp(jnp.arange(half, dtype=jnp.float32) * (-2.0 * math.log(ROPE_BASE) / HEAD_DIM))
    turned = position[..., None] * freq
    return (jnp.cos(turned), jnp.sin(turned))


def rotate(v, cosine, sine):
    half = HEAD_DIM // 2
    first = v[..., :half]
    second = v[..., half:]
    return jnp.concatenate(
        [first * cosine - second * sine, second * cosine + first * sine], axis=-1
    )


def remaining_candidates(judge_panel, duplicate_group_index, duplicate_groups):
    same = duplicate_group_index[:, None] == duplicate_group_index[None, :]
    top = jnp.max(jnp.where(same, judge_panel[None, :], -1e30), axis=1)
    expo = jnp.exp(judge_panel - top)
    total = jnp.sum(jnp.where(same, expo[None, :], 0.0), axis=1)
    weight_values = expo / total
    panel_member = (
        duplicate_group_index[:, None] == jnp.arange(duplicate_groups, dtype=jnp.int32)[None, :]
    ).astype(jnp.float32)
    return (weight_values, panel_member)


def body(
    hidden,
    lengths,
    duplicate_group_index,
    attn_gain,
    w_query,
    w_key,
    w_value,
    w_out,
    mlp_gain,
    w_gate,
    w_up,
    w_down,
    final_gain,
    reward_head,
):
    reward_judges = lax.axis_size("judge")
    devices = lax.axis_size("fsdp")
    me = lax.axis_index("fsdp")
    tokens = hidden[0]
    tok_dev, width = tokens.shape
    seq_dev = tok_dev // LEN
    cands = lengths.shape[0]
    duplicate_groups = cands // 4
    groups = width // HEAD_DIM // KV_HEADS
    column_count = width // devices
    col_start = me * column_count
    own_len = lax.dynamic_slice_in_dim(lengths, me * seq_dev, seq_dev)
    last_index = jnp.arange(seq_dev, dtype=jnp.int32) * LEN + own_len - 1
    own_last = tokens[last_index]
    x_last, gain_attn, gain_mlp = gather_packed(
        (own_last, attn_gain[0], mlp_gain[0]), "fsdp", (0, 0, 0)
    )
    gain_final = final_gain[0]
    x_last = x_last.astype(jnp.float32)
    scale = row_scale(tokens.astype(jnp.float32))
    key_rows, value_rows = sent_together((w_key[0], w_value[0]), "fsdp", 0, 1)
    tok_norm = (tokens.astype(jnp.float32) * scale * gain_attn.astype(jnp.float32)).astype(
        jnp.bfloat16
    )
    keys = jnp.dot(tok_norm, key_rows, preferred_element_type=jnp.float32)
    values = jnp.dot(tok_norm, value_rows, preferred_element_type=jnp.float32)
    key_cos, key_sin = angles(jnp.arange(LEN, dtype=jnp.float32))
    keys = keys.reshape(seq_dev, LEN, KV_HEADS, HEAD_DIM)
    keys = rotate(keys, key_cos[None, :, None, :], key_sin[None, :, None, :]).astype(jnp.bfloat16)
    values = values.astype(jnp.bfloat16).reshape(seq_dev, LEN, KV_HEADS, HEAD_DIM)
    q_norm = (x_last * row_scale(x_last) * gain_attn.astype(jnp.float32)).astype(jnp.bfloat16)
    q_part = jnp.dot(q_norm, w_query[0], preferred_element_type=jnp.float32)
    q_part = q_part.reshape(cands, q_part.shape[1] // HEAD_DIM, HEAD_DIM)
    cosine, sine = angles((lengths - 1).astype(jnp.float32))
    q_part = (
        rotate(q_part, cosine[:, None, :], sine[:, None, :]).astype(jnp.bfloat16).reshape(cands, -1)
    )
    q_own = lax.all_to_all(q_part, "fsdp", split_axis=0, concat_axis=1, tiled=True)
    q_own = q_own.reshape(seq_dev, KV_HEADS, groups, HEAD_DIM)
    scores = jnp.einsum(
        "skgd,slkd->skgl", q_own, keys, preferred_element_type=jnp.float32
    ) * HEAD_DIM ** (-0.5)
    valid = jnp.arange(LEN, dtype=jnp.int32)[None, None, None, :] < own_len[:, None, None, None]
    scores = jnp.where(valid, scores, -1e30)
    top = jnp.max(scores, axis=-1, keepdims=True)
    expo = jnp.exp(scores - top)
    probs = (expo / jnp.sum(expo, axis=-1, keepdims=True)).astype(jnp.bfloat16)
    mixed = jnp.einsum("skgl,slkd->skgd", probs, values, preferred_element_type=jnp.float32)
    mixed = mixed.reshape(seq_dev, width).astype(jnp.bfloat16)
    head_rows = lax.all_to_all(mixed, "fsdp", split_axis=1, concat_axis=0, tiled=True)
    attn = total_of(jnp.dot(head_rows, w_out[0], preferred_element_type=jnp.float32), "fsdp")
    after_attn = x_last + attn
    m_norm = (after_attn * row_scale(after_attn) * gain_mlp.astype(jnp.float32)).astype(
        jnp.bfloat16
    )
    gate = jnp.dot(m_norm, w_gate[0], preferred_element_type=jnp.float32)
    up = jnp.dot(m_norm, w_up[0], preferred_element_type=jnp.float32)
    act = (jax.nn.silu(gate) * up).astype(jnp.bfloat16)
    down_terms = jnp.dot(act, w_down[0], preferred_element_type=jnp.float32)
    down_cols = sum_at_owner(down_terms, "fsdp", 1)
    after_cols = lax.dynamic_slice_in_dim(after_attn, col_start, column_count, 1) + down_cols
    head_cols = lax.dynamic_slice_in_dim(reward_head[0], col_start, column_count, 0)
    weighted = after_cols * gain_final.astype(jnp.float32)
    squares, product = packed_total(
        (
            jnp.sum(after_cols * after_cols, axis=1),
            jnp.dot(weighted, head_cols, precision=lax.Precision.HIGHEST),
        ),
        "fsdp",
    )
    col_scale = lax.rsqrt(squares / width + EPS)
    feature_cols = weighted * col_scale[:, None]
    score = product * col_scale
    total_cols, score_total = packed_total((feature_cols, score), "judge")
    weight_values, panel_member = remaining_candidates(
        score_total / reward_judges, duplicate_group_index, duplicate_groups
    )
    cluster_cols = jnp.dot(
        panel_member.T,
        weight_values[:, None] * (total_cols / reward_judges),
        precision=lax.Precision.HIGHEST,
    )
    return (weight_values, cluster_cols)


def solution(mesh):
    in_specs = (
        P("judge", "fsdp", None),
        P(),
        P(),
        P("judge", "fsdp"),
        P("judge", None, "fsdp"),
        P("judge", "fsdp", None),
        P("judge", "fsdp", None),
        P("judge", "fsdp", None),
        P("judge", "fsdp"),
        P("judge", None, "fsdp"),
        P("judge", None, "fsdp"),
        P("judge", "fsdp", None),
        P("judge", "fsdp"),
        P("judge", None),
    )
    out_specs = (P(), P(None, "fsdp"))
    return jax.shard_map(body, mesh=mesh, in_specs=in_specs, out_specs=out_specs, check_vma=False)
```

profile of v0, /device:TPU:1, one launch (start us, length us, event | category | flops | bytes accessed | tf_op | source)
XLA Modules:
  0.0 385.3 jit_solution(3134053307039716645)
XLA Ops:
  7.2 2.0 pad_maximum_fusion
  9.2 0.7 compare_select_fusion.2
  10.0 5.0 %gather_fusion = bf16[2,4096]{1,0:T(2,128)(2,1)S(1)} fusion(bf16[1024,4096]{1,0:T(8,128)(2,1)} %bitcast.116, s32[1024]{0:T(1024)S(1)} %pad_clamp_fusion), kind=kCustom, calls=%fused_computation | custom fusion | bytes 32776 | tf_op jit(solution)/shard_map/gather | solution.py:147
  15.1 0.7 pad_maximum_fusion.2
  15.8 93.5 %all-gather.1 = bf16[32,1,8448]{2,1,0:T(2,128)(2,1)S(1)} all-gather(bf16[1,1,8448]{2,1,0:T(2,128)(2,1)S(1)} %reshape.357), channel_id=2, replica_groups=mesh['judge'=4,'fsdp'=32] {'fsdp'}, dimensions={0}, use_global_device_ids=true | all-gather | bytes 557568 | tf_op jit(solution)/shard_map/all_gather | solution.py:22
  109.4 1.1 reshape.342
  110.6 1.4 multiply_reduce_fusion.1
  112.1 0.3 mul.274
  112.5 0.6 copy.60
  113.2 0.2 convert_element_type.110
  113.4 1.6 convolution_bitcast_fusion
  115.2 0.7 pad_maximum_fusion.3
  115.9 4.0 %all-to-all-start = ((bf16[32,2,128]{2,1,0:T(2,128)(2,1)}), bf16[32,2,128]{2,1,0:T(2,128)(2,1)S(1)}, u32[]{:S(2)}, u32[]{:S(2)}) async-start(bf16[32,2,128]{2,1,0:T(2,128)(2,1)} %pad_maximum_fusion.3), calls=%async_computation | async-start | bytes 32768 | tf_op jit(solution)/shard_map/all_to_all | solution.py:171
  119.9 5.2 %fusion.1 = f32[1024]{0:T(1024)S(1)} fusion(bf16[1,1024,4096]{2,1,0:T(8,128)(2,1)} %param.14), kind=kLoop, calls=%fused_computation.4 | loop fusion | flops 12581888 | bytes 8392704 | tf_op jit(solution)/shard_map/reduce_sum | solution.py:87
  125.1 0.5 fusion.60
  125.6 10.4 %multiply_convert_fusion = bf16[1,1024,4096]{2,1,0:T(8,128)(2,1)} fusion(bf16[1,1024,4096]{2,1,0:T(8,128)(2,1)} %param.14, f32[4096]{0:T(1024)S(1)} %get-tuple-element.13, f32[1024]{0:T(1024)S(1)} %add_rsqrt_fusion.1), kind=kLoop, calls=%fused_computation.7 | loop fusion | flops 16777216 | bytes 16797696 | tf_op jit(solution)/shard_map/convert_element_type | solution.py:155
  136.1 77.0 %all-gather.4.cloned.1.call-done = bf16[4096,2048]{1,0:T(8,128)(2,1)} async-done(((bf16[128,2048]{1,0:T(8,128)(2,1)}), bf16[4096,2048]{1,0:T(8,128)(2,1)}) %all-gather.4.cloned.1.call-update) | async-done | bytes 16777232 | tf_op jit(solution)/shard_map/all_gather | solution.py:32
  213.1 7.6 %slice_bitcast_fusion = bf16[1024,4096]{0,1:T(8,128)(2,1)} fusion(bf16[4096,2048]{1,0:T(8,128)(2,1)} %all-gather.4.cloned.1.call-done), kind=kLoop, calls=%fused_computation.10 | loop fusion | bytes 16777216 | tf_op jit(solution)/shard_map/dot_general | solution.py:158
  220.7 12.0 %copy.43 = bf16[1024,4096]{1,0:T(8,128)(2,1)} copy(bf16[1024,4096]{0,1:T(8,128)(2,1)} %slice_bitcast_fusion) | data formatting | bytes 16777216 | tf_op jit(solution)/shard_map/dot_general | solution.py:158
  232.7 13.9 %convert_bitcast_fusion = bf16[128,8,8,128]{3,1,2,0:T(8,128)(2,1)S(1)} fusion(bf16[4096,2048]{1,0:T(8,128)(2,1)} %all-gather.4.cloned.1.call-done, f32[4096]{0:T(1024)S(1)} %get-tuple-element.13, f32[1024]{0:T(1024)S(1)} %add_rsqrt_fusion.1, bf16[1,1024,4096]{2,1,0:T(8,128)(2,1)} %param.14), kind=kOutput, calls=%fused_computation.26 | convolution fusion | flops 8607760384 | bytes 18894848 | tf_op jit(solution)/shard_map/dot_general | solution.py:159
  246.6 2.0 copy.62
  248.6 11.4 %fusion.103 = f32[2,512,8,128]{1,3,2,0:T(8,128)S(1)} fusion(bf16[2,512,4096,1]{2,1,3,0:T(8,128)(2,1)} %bitcast.117, bf16[8,128,4096,1]{2,1,0,3:T(8,128)(2,1)S(1)} %bitcast.118), kind=kOutput, calls=%fused_computation.122 | convolution fusion | flops 8589934592 | bytes 20971520 | tf_op jit(solution)/shard_map/dot_general | solution.py:158
  260.0 1.7 subtract_convert_fusion
  261.8 1.8 fusion.100
  263.5 2.1 fusion.46
  265.7 11.7 %all_to_all.53 = bf16[2,32,128]{2,0,1:T(2,128)(2,1)S(1)} all-to-all(bf16[2,32,128]{2,0,1:T(2,128)(2,1)S(1)} %copy.46), channel_id=1, replica_groups=mesh['judge'=4,'fsdp'=32] {'fsdp'}, dimensions={1} | all-to-all | bytes 32768 | tf_op jit(solution)/shard_map/all_to_all | solution.py:183
  277.4 0.3 fusion.49
  277.7 0.8 copy.48
  278.5 15.5 %all_to_all.54 = f32[32,2,4096]{2,1,0:T(2,128)S(1)} all-to-all(f32[32,2,4096]{2,1,0:T(2,128)S(1)} %copy.48), channel_id=1, replica_groups=mesh['judge'=4,'fsdp'=32] {'fsdp'}, dimensions={0} | all-to-all | bytes 2097152 | tf_op jit(solution)/shard_map/all_to_all | solution.py:46
  294.0 0.3 reduce_sum.93
  294.4 1.5 broadcast_in_dim.39
  295.9 7.1 %all-to-all-start.3 = ((f32[32,2,4096]{2,1,0:T(2,128)}), f32[32,2,4096]{2,1,0:T(2,128)S(1)}, u32[]{:S(2)}, u32[]{:S(2)}) async-start(f32[32,2,4096]{2,1,0:T(2,128)} %broadcast_in_dim.39), calls=%async_computation.3 | async-start | bytes 2097152 | tf_op jit(solution)/shard_map/all_to_all | solution.py:59
  303.0 1.9 reshape.344
  304.9 11.8 %all-to-all-done.3 = f32[32,2,4096]{2,1,0:T(2,128)S(1)} async-done(((f32[32,2,4096]{2,1,0:T(2,128)}), f32[32,2,4096]{2,1,0:T(2,128)S(1)}, u32[]{:S(2)}, u32[]{:S(2)}) %all-to-all-start.3) | async-done | bytes 1048608 | tf_op jit(solution)/shard_map/all_to_all | solution.py:59
  316.7 2.0 multiply_reduce_fusion
  318.6 0.6 multiply_convert_fusion.1
  319.3 0.2 convert_element_type.126
  319.5 3.2 fusion.14
  322.7 6.3 %fusion.26 = f32[32,64,128]{2,1,0:T(8,128)} fusion(bf16[64,4096]{1,0:T(8,128)(2,1)S(1)} %convert_element_type.126, bf16[1,4096,448]{1,2,0:T(8,128)(2,1)} %param.24, f32[64,448]{1,0:T(8,128)S(1)} %fusion.14, bf16[1,448,4096]{2,1,0:T(8,128)(2,1)} %param.25), kind=kOutput, calls=%fused_computation.29 | convolution fusion | flops 469934080 | bytes 9027584 | tf_op jit(solution)/shard_map/dot_general | solution.py:192
  329.0 6.7 %all-to-all-start.4 = ((f32[32,64,128]{2,1,0:T(8,128)}), f32[32,64,128]{2,1,0:T(8,128)S(1)}, u32[]{:S(2)}, u32[]{:S(2)}) async-start(f32[32,64,128]{2,1,0:T(8,128)} %fusion.26), calls=%async_computation.4 | async-start | bytes 2097152 | tf_op jit(solution)/shard_map/all_to_all | solution.py:46
  335.8 1.7 reshape.339
  337.5 13.1 %all-to-all-done.4 = f32[32,64,128]{2,1,0:T(8,128)S(1)} async-done(((f32[32,64,128]{2,1,0:T(8,128)}), f32[32,64,128]{2,1,0:T(8,128)S(1)}, u32[]{:S(2)}, u32[]{:S(2)}) %all-to-all-start.4) | async-done | bytes 1048608 | tf_op jit(solution)/shard_map/all_to_all | solution.py:46
  350.7 0.9 multiply_reduce_fusion.2
  351.6 0.8 convolution_bitcast_fusion.1
  352.5 12.5 %all_to_all.55 = f32[32,1,128]{2,1,0:T(1,128)S(1)} all-to-all(f32[32,1,128]{2,1,0:T(1,128)S(1)} %broadcast_in_dim.40), channel_id=1, replica_groups=mesh['judge'=4,'fsdp'=32] {'fsdp'}, dimensions={0} | all-to-all | bytes 32768 | tf_op jit(solution)/shard_map/all_to_all | solution.py:59
  365.3 11.2 %all_to_all.56 = f32[4,1,8256]{2,1,0:T(1,128)S(1)} all-to-all(f32[4,1,8256]{2,1,0:T(1,128)S(1)} %broadcast_in_dim.41), channel_id=1, replica_groups=mesh['judge'=4,'fsdp'=32] {'judge'}, dimensions={0} | all-to-all | bytes 264192 | tf_op jit(solution)/shard_map/all_to_all | solution.py:59
  377.1 0.5 broadcast_multiply_fusion
  377.6 0.9 fusion.74
  (46 shorter events, 1.7 us)
Async XLA Ops:
  7.2 270.2 %copy-start = (bf16[1,128,4096]{2,1,0:T(8,128)(2,1)S(1)}, bf16[1,128,4096]{2,1,0:T(8,128)(2,1)}, u32[]{:S(2)}) copy-start(bf16[1,128,4096]{2,1,0:T(8,128)(2,1)} %param.21) | copy-start | bytes 3145732
  7.2 206.0 %all-gather.4.cloned.1.call-start = ((), (), s32[]{:S(2)}) async-start(), calls=%async_computation.7 | async-start | bytes 17301504 | tf_op jit(solution)/shard_map/all_gather | solution.py:32
  112.0 3.0 copy-start.3
  115.9 20.2 %all-to-all-start = ((bf16[32,2,128]{2,1,0:T(2,128)(2,1)}), bf16[32,2,128]{2,1,0:T(2,128)(2,1)S(1)}, u32[]{:S(2)}, u32[]{:S(2)}) async-start(bf16[32,2,128]{2,1,0:T(2,128)(2,1)} %pad_maximum_fusion.3), calls=%async_computation | async-start | bytes 32768 | tf_op jit(solution)/shard_map/all_to_all | solution.py:171
  232.7 15.9 %copy-start.1 = (bf16[1024,4096]{1,0:T(8,128)(2,1)S(1)}, bf16[1024,4096]{1,0:T(8,128)(2,1)}, u32[]{:S(2)}) copy-start(bf16[1024,4096]{1,0:T(8,128)(2,1)} %copy.43) | copy-start | bytes 25165828
  295.9 20.8 %all-to-all-start.3 = ((f32[32,2,4096]{2,1,0:T(2,128)}), f32[32,2,4096]{2,1,0:T(2,128)S(1)}, u32[]{:S(2)}, u32[]{:S(2)}) async-start(f32[32,2,4096]{2,1,0:T(2,128)} %broadcast_in_dim.39), calls=%async_computation.3 | async-start | bytes 2097152 | tf_op jit(solution)/shard_map/all_to_all | solution.py:59
  322.7 13.1 %copy-start.4 = (bf16[1,128]{1,0:T(2,128)(2,1)S(1)}, bf16[1,128]{1,0:T(2,128)(2,1)}, u32[]{:S(2)}) copy-start(bf16[1,128]{1,0:T(2,128)(2,1)} %param.26) | copy-start | bytes 772
  329.0 47.6 %copy-start.2 = (s32[64]{0:T(128)S(1)}, s32[64]{0:T(128)}, u32[]{:S(2)}) copy-start(s32[64]{0:T(128)} %param.16) | copy-start | bytes 772
  329.0 21.6 %all-to-all-start.4 = ((f32[32,64,128]{2,1,0:T(8,128)}), f32[32,64,128]{2,1,0:T(8,128)S(1)}, u32[]{:S(2)}, u32[]{:S(2)}) async-start(f32[32,64,128]{2,1,0:T(8,128)} %fusion.26), calls=%async_computation.4 | async-start | bytes 2097152 | tf_op jit(solution)/shard_map/all_to_all | solution.py:46
Sparse Core Ops, SparseCore 0:
  9.6 203.4 all-gather.3
where the time goes:
time: 387 us; the launch traced here: 385 us
  blocking collectives  145 us (37%)
  waiting for transfers between devices  102 us (26%)
  matrix products  42.3 us (11%)
  local copies, waits for them, and re-layouts  35.3 us (9%)
  other arithmetic  29.1 us (8%)
  starting transfers between devices  17.9 us (5%)
  between operations  14.4 us (4%)
    all_gather x1, blocking collectives, gather_packed(): lines, at, done = (lax.all_gather(ravelled, axis), 0, [])  93.5 us
    all_gather x1, waiting for transfers between devices, sent_together(): filled, at, done = (lax.all_gather(both, axis, axis=dim, tiled=True), 0, [])  77 us
    all_to_all x2, blocking collectives, from_everyone(): lax.all_to_all(jnp.broadcast_to(x[None], (peers, *x.shape)), axis, 0, 0,...  23.8 us
    dot_general x2, local copies, waits for them, and re-layouts, body(): keys = jnp.dot(tok_norm, key_rows, preferred_element_type=jnp.float32)  19.5 us
    all_to_all x1, blocking collectives, sum_at_owner(): blocks = lax.all_to_all(cut_along(x, dim, peers), axis, 0, 0, tiled=True)  15.5 us
    dot_general x1, matrix products, body(): values = jnp.dot(tok_norm, value_rows, preferred_element_type=jnp.float32)  13.9 us
    all_to_all x1, waiting for transfers between devices, sum_at_owner(): blocks = lax.all_to_all(cut_along(x, dim, peers), axis, 0, 0, tiled=True)  13.1 us
    all_to_all x1, waiting for transfers between devices, from_everyone(): lax.all_to_all(jnp.broadcast_to(x[None], (peers, *x.shape)), axis, 0, 0,...  11.8 us
  transfers between devices with their start and end apart: 4, of which 3 were waited for; matrix products, arithmetic and copies ran while one was open for 9% of the time, Pallas kernels for 0%

commit v1 on v0

--- a/solution.py
+++ b/solution.py
@@ -180,7 +180,10 @@
     probs = (expo / jnp.sum(expo, axis=-1, keepdims=True)).astype(jnp.bfloat16)
     mixed = jnp.einsum("skgl,slkd->skgd", probs, values, preferred_element_type=jnp.float32)
     mixed = mixed.reshape(seq_dev, width).astype(jnp.bfloat16)
-    head_rows = lax.all_to_all(mixed, "fsdp", split_axis=1, concat_axis=0, tiled=True)
+    head_rows = jnp.concatenate(
+        lax.all_to_all(jnp.stack(jnp.split(mixed, lax.axis_size("fsdp"), axis=1)), "fsdp", 0, 0),
+        axis=0,
+    )
     attn = total_of(jnp.dot(head_rows, w_out[0], preferred_element_type=jnp.float32), "fsdp")
     after_attn = x_last + attn
     m_norm = (after_attn * row_scale(after_attn) * gain_mlp.astype(jnp.float32)).astype(

time: 387 us -> 389 us (level)
  transfers between devices with their start and end apart: 4 -> 4, of which waited for: 3 -> 3; matrix products, arithmetic and copies ran while one was open for 9% -> 8% of each run, Pallas kernels for 0% -> 0%
where the time goes in v1:
time: 389 us; the launch traced here: 388 us
  blocking collectives  145 us (37%)
  waiting for transfers between devices  102 us (26%)
  matrix products  42.3 us (11%)
  local copies, waits for them, and re-layouts  36.6 us (9%)
  other arithmetic  29.8 us (8%)
  starting transfers between devices  17.9 us (5%)
  between operations  14.5 us (4%)
    all_gather x1, blocking collectives, gather_packed(): lines, at, done = (lax.all_gather(ravelled, axis), 0, [])  93.5 us
    all_gather x1, waiting for transfers between devices, sent_together(): filled, at, done = (lax.all_gather(both, axis, axis=dim, tiled=True), 0, [])  77 us
    all_to_all x2, blocking collectives, from_everyone(): lax.all_to_all(jnp.broadcast_to(x[None], (peers, *x.shape)), axis, 0, 0,...  23.8 us
    dot_general x2, local copies, waits for them, and re-layouts, body(): keys = jnp.dot(tok_norm, key_rows, preferred_element_type=jnp.float32)  19.5 us
    all_to_all x1, blocking collectives, sum_at_owner(): blocks = lax.all_to_all(cut_along(x, dim, peers), axis, 0, 0, tiled=True)  15.5 us
    dot_general x1, matrix products, body(): values = jnp.dot(tok_norm, value_rows, preferred_element_type=jnp.float32)  13.9 us
    all_to_all x1, waiting for transfers between devices, sum_at_owner(): blocks = lax.all_to_all(cut_along(x, dim, peers), axis, 0, 0, tiled=True)  13.1 us
    all_to_all x1, waiting for transfers between devices, from_everyone(): lax.all_to_all(jnp.broadcast_to(x[None], (peers, *x.shape)), axis, 0, 0,...  11.8 us
  transfers between devices with their start and end apart: 4, of which 3 were waited for; matrix products, arithmetic and copies ran while one was open for 8% of the time, Pallas kernels for 0%

profile of v1, /device:TPU:1, one launch (start us, length us, event | category | flops | bytes accessed | tf_op | source)
XLA Modules:
  0.0 387.5 jit_solution(8945673412101251983)
XLA Ops:
  7.2 2.0 pad_maximum_fusion
  9.2 0.7 compare_select_fusion.2
  10.0 5.0 %gather_fusion = bf16[2,4096]{1,0:T(2,128)(2,1)S(1)} fusion(bf16[1024,4096]{1,0:T(8,128)(2,1)} %bitcast.242, s32[1024]{0:T(1024)S(1)} %pad_clamp_fusion), kind=kCustom, calls=%fused_computation | custom fusion | bytes 32776 | tf_op jit(solution)/shard_map/gather | solution.py:147
  15.1 0.7 pad_maximum_fusion.2
  15.8 93.5 %all-gather.1 = bf16[32,1,8448]{2,1,0:T(2,128)(2,1)S(1)} all-gather(bf16[1,1,8448]{2,1,0:T(2,128)(2,1)S(1)} %reshape_bitcast_fusion), channel_id=2, replica_groups=mesh['judge'=4,'fsdp'=32] {'fsdp'}, dimensions={0}, use_global_device_ids=true | all-gather | bytes 557568 | tf_op jit(solution)/shard_map/all_gather | solution.py:22
  109.4 1.1 reshape.339
  110.6 1.4 multiply_reduce_fusion.1
  112.1 0.3 mul.274
  112.5 0.6 copy.1203
  113.2 0.2 convert_element_type.109
  113.4 1.6 convolution_bitcast_fusion
  115.2 0.7 pad_maximum_fusion.3
  115.9 4.0 %all-to-all-start = ((bf16[32,2,128]{2,1,0:T(2,128)(2,1)}), bf16[32,2,128]{2,1,0:T(2,128)(2,1)S(1)}, u32[]{:S(2)}, u32[]{:S(2)}) async-start(bf16[32,2,128]{2,1,0:T(2,128)(2,1)} %pad_maximum_fusion.3), calls=%async_computation | async-start | bytes 32768 | tf_op jit(solution)/shard_map/all_to_all | solution.py:171
  119.9 5.2 %fusion.1 = f32[1024]{0:T(1024)S(1)} fusion(bf16[1,1024,4096]{2,1,0:T(8,128)(2,1)} %param.14), kind=kLoop, calls=%fused_computation.4 | loop fusion | flops 12581888 | bytes 8392704 | tf_op jit(solution)/shard_map/reduce_sum | solution.py:87
  125.1 0.5 fusion.60
  125.6 10.4 %multiply_convert_fusion = bf16[1,1024,4096]{2,1,0:T(8,128)(2,1)} fusion(bf16[1,1024,4096]{2,1,0:T(8,128)(2,1)} %param.14, f32[4096]{0:T(1024)S(1)} %get-tuple-element.13, f32[1024]{0:T(1024)S(1)} %add_rsqrt_fusion.1), kind=kLoop, calls=%fused_computation.7 | loop fusion | flops 16777216 | bytes 16797696 | tf_op jit(solution)/shard_map/convert_element_type | solution.py:155
  136.1 77.0 %all-gather.4.cloned.1.call-done = bf16[4096,2048]{1,0:T(8,128)(2,1)} async-done(((bf16[128,2048]{1,0:T(8,128)(2,1)}), bf16[4096,2048]{1,0:T(8,128)(2,1)}) %all-gather.4.cloned.1.call-update) | async-done | bytes 16777232 | tf_op jit(solution)/shard_map/all_gather | solution.py:32
  213.1 7.6 %slice_bitcast_fusion = bf16[1024,4096]{0,1:T(8,128)(2,1)} fusion(bf16[4096,2048]{1,0:T(8,128)(2,1)} %all-gather.4.cloned.1.call-done), kind=kLoop, calls=%fused_computation.10 | loop fusion | bytes 16777216 | tf_op jit(solution)/shard_map/dot_general | solution.py:158
  220.7 12.0 %copy.1187 = bf16[1024,4096]{1,0:T(8,128)(2,1)} copy(bf16[1024,4096]{0,1:T(8,128)(2,1)} %slice_bitcast_fusion) | data formatting | bytes 16777216 | tf_op jit(solution)/shard_map/dot_general | solution.py:158
  232.7 13.9 %convert_bitcast_fusion = bf16[128,8,8,128]{3,1,2,0:T(8,128)(2,1)S(1)} fusion(bf16[4096,2048]{1,0:T(8,128)(2,1)} %all-gather.4.cloned.1.call-done, f32[4096]{0:T(1024)S(1)} %get-tuple-element.13, f32[1024]{0:T(1024)S(1)} %add_rsqrt_fusion.1, bf16[1,1024,4096]{2,1,0:T(8,128)(2,1)} %param.14), kind=kOutput, calls=%fused_computation.26 | convolution fusion | flops 8607760384 | bytes 18894848 | tf_op jit(solution)/shard_map/dot_general | solution.py:159
  246.6 2.0 copy.1205
  248.6 11.4 %fusion.102 = f32[2,512,8,128]{1,3,2,0:T(8,128)S(1)} fusion(bf16[2,512,4096,1]{2,1,3,0:T(8,128)(2,1)} %bitcast.243, bf16[8,128,4096,1]{2,1,0,3:T(8,128)(2,1)S(1)} %bitcast.244), kind=kOutput, calls=%fused_computation.186 | convolution fusion | flops 8589934592 | bytes 20971520 | tf_op jit(solution)/shard_map/dot_general | solution.py:158
  260.0 1.7 subtract_convert_fusion
  261.8 1.8 fusion.99
  263.5 2.1 fusion.46
  266.0 11.7 %all_to_all.45 = bf16[32,2,128]{2,1,0:T(2,128)(2,1)S(1)} all-to-all(bf16[32,2,128]{2,1,0:T(2,128)(2,1)S(1)} %constant_dynamic-update-slice_fusion), channel_id=1, replica_groups=mesh['judge'=4,'fsdp'=32] {'fsdp'}, dimensions={0} | all-to-all | bytes 32768 | tf_op jit(solution)/shard_map/all_to_all | solution.py:184
  277.8 0.3 fusion.49
  278.1 0.8 copy.1191
  278.9 15.5 %all_to_all.46 = f32[32,2,4096]{2,1,0:T(2,128)S(1)} all-to-all(f32[32,2,4096]{2,1,0:T(2,128)S(1)} %copy.1191), channel_id=1, replica_groups=mesh['judge'=4,'fsdp'=32] {'fsdp'}, dimensions={0} | all-to-all | bytes 2097152 | tf_op jit(solution)/shard_map/all_to_all | solution.py:46
  294.4 0.3 reduce_sum.93
  294.8 1.5 broadcast_in_dim.39
  296.3 7.1 %all-to-all-start.3 = ((f32[32,2,4096]{2,1,0:T(2,128)}), f32[32,2,4096]{2,1,0:T(2,128)S(1)}, u32[]{:S(2)}, u32[]{:S(2)}) async-start(f32[32,2,4096]{2,1,0:T(2,128)} %broadcast_in_dim.39), calls=%async_computation.3 | async-start | bytes 2097152 | tf_op jit(solution)/shard_map/all_to_all | solution.py:59
  303.4 1.9 reshape.341
  305.3 11.8 %all-to-all-done.3 = f32[32,2,4096]{2,1,0:T(2,128)S(1)} async-done(((f32[32,2,4096]{2,1,0:T(2,128)}), f32[32,2,4096]{2,1,0:T(2,128)S(1)}, u32[]{:S(2)}, u32[]{:S(2)}) %all-to-all-start.3) | async-done | bytes 1048608 | tf_op jit(solution)/shard_map/all_to_all | solution.py:59
  317.0 2.0 multiply_reduce_fusion
  319.0 1.4 multiply_convert_fusion.1
  320.4 1.2 convert_element_type.125
  321.7 3.2 fusion.14
  324.9 6.3 %fusion.26 = f32[32,64,128]{2,1,0:T(8,128)} fusion(bf16[64,4096]{1,0:T(8,128)(2,1)S(1)} %convert_element_type.125, bf16[1,4096,448]{1,2,0:T(8,128)(2,1)} %param.24, f32[64,448]{1,0:T(8,128)S(1)} %fusion.14, bf16[1,448,4096]{2,1,0:T(8,128)(2,1)} %param.25), kind=kOutput, calls=%fused_computation.29 | convolution fusion | flops 469934080 | bytes 9027584 | tf_op jit(solution)/shard_map/dot_general | solution.py:195
  331.2 6.7 %all-to-all-start.4 = ((f32[32,64,128]{2,1,0:T(8,128)}), f32[32,64,128]{2,1,0:T(8,128)S(1)}, u32[]{:S(2)}, u32[]{:S(2)}) async-start(f32[32,64,128]{2,1,0:T(8,128)} %fusion.26), calls=%async_computation.4 | async-start | bytes 2097152 | tf_op jit(solution)/shard_map/all_to_all | solution.py:46
  338.0 1.7 reshape.336
  339.7 13.1 %all-to-all-done.4 = f32[32,64,128]{2,1,0:T(8,128)S(1)} async-done(((f32[32,64,128]{2,1,0:T(8,128)}), f32[32,64,128]{2,1,0:T(8,128)S(1)}, u32[]{:S(2)}, u32[]{:S(2)}) %all-to-all-start.4) | async-done | bytes 1048608 | tf_op jit(solution)/shard_map/all_to_all | solution.py:46
  352.9 0.9 multiply_reduce_fusion.2
  353.8 0.8 convolution_bitcast_fusion.1
  354.7 12.5 %all_to_all.47 = f32[32,1,128]{2,1,0:T(1,128)S(1)} all-to-all(f32[32,1,128]{2,1,0:T(1,128)S(1)} %broadcast_in_dim.40), channel_id=1, replica_groups=mesh['judge'=4,'fsdp'=32] {'fsdp'}, dimensions={0} | all-to-all | bytes 32768 | tf_op jit(solution)/shard_map/all_to_all | solution.py:59
  367.5 11.2 %all_to_all.48 = f32[4,1,8256]{2,1,0:T(1,128)S(1)} all-to-all(f32[4,1,8256]{2,1,0:T(1,128)S(1)} %broadcast_in_dim.41), channel_id=1, replica_groups=mesh['judge'=4,'fsdp'=32] {'judge'}, dimensions={0} | all-to-all | bytes 264192 | tf_op jit(solution)/shard_map/all_to_all | solution.py:59
  379.3 0.5 broadcast_multiply_fusion
  379.8 0.9 fusion.74
  (78 shorter events, 2.0 us)
Async XLA Ops:
  7.2 270.6 %copy-start = (bf16[1,128,4096]{2,1,0:T(8,128)(2,1)S(1)}, bf16[1,128,4096]{2,1,0:T(8,128)(2,1)}, u32[]{:S(2)}) copy-start(bf16[1,128,4096]{2,1,0:T(8,128)(2,1)} %param.21) | copy-start | bytes 3145732
  7.2 206.0 %all-gather.4.cloned.1.call-start = ((), (), s32[]{:S(2)}) async-start(), calls=%async_computation.7 | async-start | bytes 17301504 | tf_op jit(solution)/shard_map/all_gather | solution.py:32
  112.0 3.0 copy-start.3
  115.9 20.2 %all-to-all-start = ((bf16[32,2,128]{2,1,0:T(2,128)(2,1)}), bf16[32,2,128]{2,1,0:T(2,128)(2,1)S(1)}, u32[]{:S(2)}, u32[]{:S(2)}) async-start(bf16[32,2,128]{2,1,0:T(2,128)(2,1)} %pad_maximum_fusion.3), calls=%async_computation | async-start | bytes 32768 | tf_op jit(solution)/shard_map/all_to_all | solution.py:171
  232.7 15.9 %copy-start.1 = (bf16[1024,4096]{1,0:T(8,128)(2,1)S(1)}, bf16[1024,4096]{1,0:T(8,128)(2,1)}, u32[]{:S(2)}) copy-start(bf16[1024,4096]{1,0:T(8,128)(2,1)} %copy.1187) | copy-start | bytes 25165828
  296.3 20.8 %all-to-all-start.3 = ((f32[32,2,4096]{2,1,0:T(2,128)}), f32[32,2,4096]{2,1,0:T(2,128)S(1)}, u32[]{:S(2)}, u32[]{:S(2)}) async-start(f32[32,2,4096]{2,1,0:T(2,128)} %broadcast_in_dim.39), calls=%async_computation.3 | async-start | bytes 2097152 | tf_op jit(solution)/shard_map/all_to_all | solution.py:59
  324.9 13.1 %copy-start.4 = (bf16[1,128]{1,0:T(2,128)(2,1)S(1)}, bf16[1,128]{1,0:T(2,128)(2,1)}, u32[]{:S(2)}) copy-start(bf16[1,128]{1,0:T(2,128)(2,1)} %param.26) | copy-start | bytes 772
  331.2 47.6 %copy-start.2 = (s32[64]{0:T(128)S(1)}, s32[64]{0:T(128)}, u32[]{:S(2)}) copy-start(s32[64]{0:T(128)} %param.16) | copy-start | bytes 772
  331.2 21.6 %all-to-all-start.4 = ((f32[32,64,128]{2,1,0:T(8,128)}), f32[32,64,128]{2,1,0:T(8,128)S(1)}, u32[]{:S(2)}, u32[]{:S(2)}) async-start(f32[32,64,128]{2,1,0:T(8,128)} %fusion.26), calls=%async_computation.4 | async-start | bytes 2097152 | tf_op jit(solution)/shard_map/all_to_all | solution.py:46
Sparse Core Ops, SparseCore 0:
  9.6 203.4 all-gather.3
